TPU v7x, 512 devices: a whole 4x4x16 slice. The times are simulated.
512 devices in a mesh: expert: 32 (over z_hi, x, core), row: 4 (over z_lo), col: 4 (over y).
Axes of the slice: x: 4, y: 4, z: 16 (z_hi: 4, z_lo: 4; z = z_hi * 4 + z_lo), core: 2. Of those that a mesh axis runs over, the one named last changes fastest.
Arguments:
- tokens: bfloat16 [32768, 3584], P(('expert', 'col'), 'row'), may hold values from -6 to 6
- slots: int32 [128, 6, 32, 2], P(('expert', 'col')), may hold values from 0 to 255
- counts: int32 [6, 32], replicated, may hold values from 1 to 256, as said below
- owner: int32 [32], replicated, may hold values from 0 to 31, each once
Outputs:
- moments: float32 [32, 3584, 3584], P('expert', 'row', 'col')
Inputs may be any that keep to these rules, and one draw needn't show every extreme that they name: `counts`: in every panel at least one expert's count is 256.
All inputs are finite; a program needn't handle non-finite values.
Results may differ from a plain program's by a relative error of at most 0.0003.
Values may be sent and summed in bfloat16 or wider, within the bound.
No kernel may reach another device: no remote copies, remote signals or barrier semaphores. Data moves between devices by JAX's collectives and lax.ppermute only.
A program may use at most 64 MiB of HBM per device.

v0:
```python
import jax
import jax.numpy as jnp
from jax import lax
from jax.sharding import PartitionSpec as P


def from_root(value, axis, root):
    mine = lax.axis_index(axis) == root
    return lax.psum(jnp.where(mine, value, jnp.zeros_like(value)), axis)


def panel_moment(outgoing):
    received = lax.all_to_all(outgoing, "expert", split_axis=1, concat_axis=1, tiled=True)
    panel_count = received.shape[0]
    feature_count = received.shape[3]
    left_rows = lax.all_gather(received, "col", axis=2, tiled=True)
    left_rows = left_rows.reshape(panel_count, -1, feature_count)
    right_rows = from_root(left_rows, "row", lax.axis_index("col"))
    return jnp.einsum("kpa,kpb->ab", left_rows, right_rows, preferred_element_type=jnp.float32)


def per_device(tokens, slots, counts, owner):
    col_count = lax.axis_size("col")
    slot_count = slots.shape[3]
    block_index = lax.axis_index("expert") * col_count + lax.axis_index("col")
    inverse = jnp.argsort(owner)
    dest_slots = jnp.take(slots[0], inverse, axis=1)
    dest_counts = jnp.take(counts, inverse, axis=1)
    position = block_index * slot_count + jnp.arange(slot_count, dtype=jnp.int32)
    usable = position[None, None, :] < dest_counts[:, :, None]
    picked = tokens[dest_slots]
    outgoing = jnp.where(usable[..., None], picked, jnp.zeros_like(picked))
    own_expert = inverse[lax.axis_index("expert")]
    row_total = jnp.sum(jnp.take(counts, own_expert, axis=1)).astype(jnp.float32)
    moment_tile = jnp.zeros((tokens.shape[1], tokens.shape[1]), jnp.float32)
    for panel in range(outgoing.shape[0]):
        moment_tile = moment_tile + panel_moment(outgoing[panel : panel + 1])
    return (moment_tile / row_total)[None]


def solution(mesh):
    return jax.shard_map(
        per_device,
        mesh=mesh,
        in_specs=(P(("expert", "col"), "row"), P(("expert", "col"), None, None, None), P(), P()),
        out_specs=P("expert", "row", "col"),
        check_vma=False,
    )
```

profile of v0, /device:TPU:1, one launch (start us, length us, event | category | flops | bytes accessed | tf_op | source)
XLA Modules:
  0.0 362.5 jit_solution(1238533840400708526)
XLA Ops:
  6.5 0.0 copy-start
  6.5 2.3 sort.17
  8.9 0.8 copy.21
  9.7 0.8 copy.22
  10.5 0.6 gather_fusion
  11.0 0.6 gather_fusion.1
  11.6 0.1 select_bitcast_fusion.6
  11.7 0.1 compare_select_fusion
  11.8 0.4 copy.23
  12.2 0.1 reshape.248
  12.3 2.3 gather_fusion.2
  14.6 0.3 reshape.247
  14.9 0.1 broadcast_compare_fusion
  15.0 0.8 broadcast_select_fusion
  15.8 1.2 fusion.17
  17.0 35.4 %all_to_all.30 = bf16[1,32,2,896]{3,2,0,1:T(2,128)(2,1)S(1)} all-to-all(bf16[1,32,2,896]{3,2,0,1:T(2,128)(2,1)S(1)} %get-tuple-element.25), channel_id=1, replica_groups=mesh['expert'=32,'row'=4,'col'=4] {'expert'}, dimensions={1} | all-to-all | bytes 229376 | tf_op jit(solution)/shard_map/all_to_all | solution.py:13
  52.4 20.9 %all_to_all.31 = bf16[1,32,2,896]{3,2,0,1:T(2,128)(2,1)S(1)} all-to-all(bf16[1,32,2,896]{3,2,0,1:T(2,128)(2,1)S(1)} %get-tuple-element.26), channel_id=1, replica_groups=mesh['expert'=32,'row'=4,'col'=4] {'expert'}, dimensions={1} | all-to-all | bytes 229376 | tf_op jit(solution)/shard_map/all_to_all | solution.py:13
  73.3 20.9 %all_to_all.32 = bf16[1,32,2,896]{3,2,0,1:T(2,128)(2,1)S(1)} all-to-all(bf16[1,32,2,896]{3,2,0,1:T(2,128)(2,1)S(1)} %get-tuple-element.28), channel_id=1, replica_groups=mesh['expert'=32,'row'=4,'col'=4] {'expert'}, dimensions={1} | all-to-all | bytes 229376 | tf_op jit(solution)/shard_map/all_to_all | solution.py:13
  94.3 20.9 %all_to_all.33 = bf16[1,32,2,896]{3,2,0,1:T(2,128)(2,1)S(1)} all-to-all(bf16[1,32,2,896]{3,2,0,1:T(2,128)(2,1)S(1)} %get-tuple-element.29), channel_id=1, replica_groups=mesh['expert'=32,'row'=4,'col'=4] {'expert'}, dimensions={1} | all-to-all | bytes 229376 | tf_op jit(solution)/shard_map/all_to_all | solution.py:13
  115.2 5.1 %all-to-all-start.2 = ((bf16[1,32,2,896]{3,2,0,1:T(2,128)(2,1)}), bf16[1,32,2,896]{3,2,0,1:T(2,128)(2,1)S(1)}, u32[]{:S(2)}, u32[]{:S(2)}) async-start(bf16[1,32,2,896]{3,2,0,1:T(2,128)(2,1)} %get-tuple-element.27), calls=%async_computation.2 | async-start | bytes 229376 | tf_op jit(solution)/shard_map/all_to_all | solution.py:13
  120.4 11.2 %all_gather.18 = bf16[1,32,8,896]{3,1,0,2:T(8,128)(2,1)S(1)} all-gather(bf16[1,32,2,896]{3,1,0,2:T(8,128)(2,1)S(1)} %copy.25), channel_id=1, replica_groups=mesh['expert'=32,'row'=4,'col'=4] {'col'}, dimensions={2}, use_global_device_ids=true | all-gather | bytes 573440 | tf_op jit(solution)/shard_map/all_gather | solution.py:16
  131.6 10.0 %all_gather.19 = bf16[1,32,8,896]{3,1,0,2:T(8,128)(2,1)S(1)} all-gather(bf16[1,32,2,896]{3,1,0,2:T(8,128)(2,1)S(1)} %copy.28), channel_id=1, replica_groups=mesh['expert'=32,'row'=4,'col'=4] {'col'}, dimensions={2}, use_global_device_ids=true | all-gather | bytes 573440 | tf_op jit(solution)/shard_map/all_gather | solution.py:16
  141.7 0.0 all-to-all-done.2
  141.7 19.5 %all-to-all-start.5 = ((bf16[1,32,2,896]{3,2,0,1:T(2,128)(2,1)}), bf16[1,32,2,896]{3,2,0,1:T(2,128)(2,1)S(1)}, u32[]{:S(2)}, u32[]{:S(2)}) async-start(bf16[1,32,2,896]{3,2,0,1:T(2,128)(2,1)} %get-tuple-element.24), calls=%async_computation.5 | async-start | bytes 229376 | tf_op jit(solution)/shard_map/all_to_all | solution.py:13
  161.2 0.0 all-reduce.3.cloned.1.call-start
  161.2 10.8 %all_gather.20 = bf16[1,32,8,896]{3,1,0,2:T(8,128)(2,1)S(1)} all-gather(bf16[1,32,2,896]{3,1,0,2:T(8,128)(2,1)S(1)} %copy.31), channel_id=1, replica_groups=mesh['expert'=32,'row'=4,'col'=4] {'col'}, dimensions={2}, use_global_device_ids=true | all-gather | bytes 573440 | tf_op jit(solution)/shard_map/all_gather | solution.py:16
  172.1 10.0 %all_gather.21 = bf16[1,32,8,896]{3,1,0,2:T(8,128)(2,1)S(1)} all-gather(bf16[1,32,2,896]{3,1,0,2:T(8,128)(2,1)S(1)} %copy.34), channel_id=1, replica_groups=mesh['expert'=32,'row'=4,'col'=4] {'col'}, dimensions={2}, use_global_device_ids=true | all-gather | bytes 573440 | tf_op jit(solution)/shard_map/all_gather | solution.py:16
  182.1 10.6 %all_gather.22 = bf16[1,32,8,896]{3,1,0,2:T(8,128)(2,1)S(1)} all-gather(bf16[1,32,2,896]{3,1,0,2:T(8,128)(2,1)S(1)} %copy.37), channel_id=1, replica_groups=mesh['expert'=32,'row'=4,'col'=4] {'col'}, dimensions={2}, use_global_device_ids=true | all-gather | bytes 573440 | tf_op jit(solution)/shard_map/all_gather | solution.py:16
  192.7 0.0 all-to-all-done.5
  192.7 10.8 %all_gather.23 = bf16[1,32,8,896]{3,1,0,2:T(8,128)(2,1)S(1)} all-gather(bf16[1,32,2,896]{3,1,0,2:T(8,128)(2,1)S(1)} %copy.40), channel_id=1, replica_groups=mesh['expert'=32,'row'=4,'col'=4] {'col'}, dimensions={2}, use_global_device_ids=true | all-gather | bytes 573440 | tf_op jit(solution)/shard_map/all_gather | solution.py:16
  203.6 1.0 select_bitcast_fusion
  204.5 0.9 select_bitcast_fusion.1
  205.5 1.0 select_bitcast_fusion.2
  206.4 0.9 select_bitcast_fusion.3
  207.3 0.9 select_bitcast_fusion.4
  208.3 1.0 select_bitcast_fusion.5
  209.2 0.0 all-reduce.3.cloned.1.call-update
  209.3 0.6 dynamic_slice.3
  211.8 0.0 copy-done.6
  211.8 0.7 select_reduce_fusion
  213.2 135.0 %all-reduce.3.cloned.1.call-done = (bf16[256,896]{1,0:T(8,128)(2,1)}, bf16[256,896]{1,0:T(8,128)(2,1)}, bf16[256,896]{1,0:T(8,128)(2,1)}, bf16[256,896]{1,0:T(8,...) async-done(((bf16[256,896]{1,0:T(8,128)(2,1)}, bf16[256,896]{1,0:T(8,128)(2,1)}, bf16[256,896]{1,0:T(8,128)(2,1)}, bf16[256,896]{1,0:T(8,128)(2,1)}, ...) | async-done | bytes 2752528 | tf_op jit(solution)/shard_map/psum | solution.py:9
  348.1 1.8 fusion.1
  349.9 0.7 fusion.3
  350.6 0.7 fusion.5
  351.3 0.7 fusion.9
  352.0 0.7 fusion.7
  352.7 0.0 copy-done.1
  352.7 2.9 divide_bitcast_fusion
  (23 shorter events, 0.1 us)
Async XLA Ops:
  6.5 5.8 %copy-start = (bf16[256,896]{1,0:T(8,128)(2,1)S(1)}, bf16[256,896]{1,0:T(8,128)(2,1)}, u32[]{:S(2)}) copy-start(bf16[256,896]{1,0:T(8,128)(2,1)} %param.4) | copy-start | bytes 1376260
  115.2 26.5 %all-to-all-start.2 = ((bf16[1,32,2,896]{3,2,0,1:T(2,128)(2,1)}), bf16[1,32,2,896]{3,2,0,1:T(2,128)(2,1)S(1)}, u32[]{:S(2)}, u32[]{:S(2)}) async-start(bf16[1,32,2,896]{3,2,0,1:T(2,128)(2,1)} %get-tuple-element.27), calls=%async_computation.2 | async-start | bytes 229376 | tf_op jit(solution)/shard_map/all_to_all | solution.py:13
  141.7 51.0 %all-to-all-start.5 = ((bf16[1,32,2,896]{3,2,0,1:T(2,128)(2,1)}), bf16[1,32,2,896]{3,2,0,1:T(2,128)(2,1)S(1)}, u32[]{:S(2)}, u32[]{:S(2)}) async-start(bf16[1,32,2,896]{3,2,0,1:T(2,128)(2,1)} %get-tuple-element.24), calls=%async_computation.5 | async-start | bytes 229376 | tf_op jit(solution)/shard_map/all_to_all | solution.py:13
  161.2 187.0 %all-reduce.3.cloned.1.call-start = ((), (), s32[]{:S(2)}) async-start(), calls=%async_computation.6 | async-start | bytes 5505024 | tf_op jit(solution)/shard_map/psum | solution.py:9
  205.5 6.3 %copy-start.6 = (s32[6,32]{1,0:T(8,128)S(1)}, s32[6,32]{1,0:T(8,128)}, u32[]{:S(2)}) copy-start(s32[6,32]{1,0:T(8,128)} %param.6) | copy-start | bytes 2308
  348.1 1.8 copy-start.5
  348.1 2.5 copy-start.4
  349.9 1.4 copy-start.3
  350.6 1.4 copy-start.2
  351.3 1.4 copy-start.1
Sparse Core Ops, SparseCore 0:
  209.4 138.7 all-reduce.2
where the time goes:
time: 363 us
  blocking collectives  162 us (45%)
  waiting for transfers between devices  135 us (37%)
  starting transfers between devices  24.6 us (7%)
  between operations  16.2 us (4%)
  other arithmetic  9.83 us (3%)
  local copies, waits for them, and re-layouts  7.67 us (2%)
  matrix products  7.42 us (2%)
    psum x1, waiting for transfers between devices, from_root(): return lax.psum(jnp.where(mine, value, jnp.zeros_like(value)), axis)  135 us
    all_to_all x4, blocking collectives, panel_moment(): lax.all_to_all(outgoing, 'expert', split_axis=1, concat_axis=1, tiled=True)  98.2 us
    all_gather x6, blocking collectives, panel_moment(): left_rows = lax.all_gather(received, 'col', axis=2, tiled=True)  63.5 us
    all_to_all x2, starting transfers between devices, panel_moment(): lax.all_to_all(outgoing, 'expert', split_axis=1, concat_axis=1, tiled=True)  24.6 us
    dot_general x6, matrix products, panel_moment(): jnp.einsum('kpa,kpb->ab', left_rows, right_rows, preferred_element_type=j...  7.42 us
  transfers between devices with their start and end apart: 3, of which 1 were waited for; matrix products, arithmetic and copies ran while one was open for 0% of the time, Pallas kernels for 0%

commit v1 on v0

--- a/solution.py
+++ b/solution.py
@@ -6,7 +6,7 @@
 
 def from_root(value, axis, root):
     mine = lax.axis_index(axis) == root
-    return lax.psum(jnp.where(mine, value, jnp.zeros_like(value)), axis)
+    return jnp.sum(lax.all_gather(jnp.where(mine, value, jnp.zeros_like(value)), axis), axis=0)
 
 
 def panel_moment(outgoing):

time: 363 us -> 404 us (1.11)
  blocking collectives: 162 us -> 178 us
  other arithmetic: 9.83 us -> 25.2 us
  matrix products: 7.42 us -> 21.3 us
  starting transfers between devices: 24.6 us -> 19.4 us
    psum x1 -> x0, waiting for transfers between devices: 135 us -> none  [from_root(): return lax.psum(jnp.where(mine, value, jnp.zeros_like(value)), axis)]
    all_gather x0 -> x6, waiting for transfers between devices: none -> 119 us  [from_root(): lax.all_gather(jnp.where(mine, value, jnp.zeros_like(value)), axis)]
    all_to_all x2 -> x1, waiting for transfers between devices: 0.01 us -> 16.4 us  [panel_moment(): lax.all_to_all(outgoing, 'expert', split_axis=1, concat_axis=1, tiled=True)]
    reduce_sum x0 -> x6, other arithmetic: none -> 15.4 us  [from_root(): jnp.sum(lax.all_gather(jnp.where(mine, value, jnp.zeros_like(value)), axi...]
    dot_general x6, matrix products: 7.42 us -> 21.3 us  [panel_moment(): jnp.einsum('kpa,kpb->ab', left_rows, right_rows, preferred_element_type=j...]
    all_to_all x4 -> x5, blocking collectives: 98.2 us -> 112 us  [panel_moment(): lax.all_to_all(outgoing, 'expert', split_axis=1, concat_axis=1, tiled=True)]
    select_n x0 -> x6, other arithmetic: none -> 5.68 us  [from_root(): jnp.where(mine, value, jnp.zeros_like(value))]
    another operation x6 -> x0, other arithmetic: 5.66 us -> none
  transfers between devices with their start and end apart: 3 -> 7, of which waited for: 1 -> 4; matrix products, arithmetic and copies ran while one was open for 0% -> 8% of each run, Pallas kernels for 0% -> 0%
where the time goes in v1:
time: 404 us; the launch traced here: 403 us
  blocking collectives  178 us (44%)
  waiting for transfers between devices  135 us (33%)
  other arithmetic  25.2 us (6%)
  matrix products  21.3 us (5%)
  starting transfers between devices  19.4 us (5%)
  between operations  15.8 us (4%)
  local copies, waits for them, and re-layouts  7.57 us (2%)
    all_gather x6, waiting for transfers between devices, from_root(): lax.all_gather(jnp.where(mine, value, jnp.zeros_like(value)), axis)  119 us
    all_to_all x5, blocking collectives, panel_moment(): lax.all_to_all(outgoing, 'expert', split_axis=1, concat_axis=1, tiled=True)  112 us
    all_gather x6, blocking collectives, panel_moment(): left_rows = lax.all_gather(received, 'col', axis=2, tiled=True)  66.9 us
    dot_general x6, matrix products, panel_moment(): jnp.einsum('kpa,kpb->ab', left_rows, right_rows, preferred_element_type=j...  21.3 us
    all_to_all x1, starting transfers between devices, panel_moment(): lax.all_to_all(outgoing, 'expert', split_axis=1, concat_axis=1, tiled=True)  19.2 us
    all_to_all x1, waiting for transfers between devices, panel_moment(): lax.all_to_all(outgoing, 'expert', split_axis=1, concat_axis=1, tiled=True)  16.4 us
    reduce_sum x6, other arithmetic, from_root(): jnp.sum(lax.all_gather(jnp.where(mine, value, jnp.zeros_like(value)), axi...  15.4 us
  transfers between devices with their start and end apart: 7, of which 4 were waited for; matrix products, arithmetic and copies ran while one was open for 8% of the time, Pallas kernels for 0%

profile of v1, /device:TPU:1, one launch (start us, length us, event | category | flops | bytes accessed | tf_op | source)
XLA Modules:
  0.0 402.9 jit_solution(12316746823402091416)
XLA Ops:
  6.5 2.3 sort.17
  8.9 0.8 copy.21
  9.7 0.8 copy.22
  10.5 0.6 gather_fusion
  11.0 0.6 gather_fusion.1
  11.7 0.1 compare_select_fusion
  11.8 0.4 copy.23
  12.2 0.1 reshape.242
  12.3 2.3 gather_fusion.2
  14.6 0.3 reshape.241
  15.0 0.8 broadcast_select_fusion
  15.8 1.1 fusion.17
  17.0 19.2 %all-to-all-start.4 = ((bf16[1,32,2,896]{3,2,0,1:T(2,128)(2,1)}), bf16[1,32,2,896]{3,2,0,1:T(2,128)(2,1)S(1)}, u32[]{:S(2)}, u32[]{:S(2)}) async-start(bf16[1,32,2,896]{3,2,0,1:T(2,128)(2,1)} %get-tuple-element.19), calls=%async_computation.4 | async-start | bytes 229376 | tf_op jit(solution)/shard_map/all_to_all | solution.py:13
  36.2 16.4 %all-to-all-done.4 = bf16[1,32,2,896]{3,2,0,1:T(2,128)(2,1)S(1)} async-done(((bf16[1,32,2,896]{3,2,0,1:T(2,128)(2,1)}), bf16[1,32,2,896]{3,2,0,1:T(2,128)(2,1)S(1)}, u32[]{:S(2)}, u32[]{:S(2)}) %all-to-all-start.4) | async-done | bytes 114720 | tf_op jit(solution)/shard_map/all_to_all | solution.py:13
  52.6 11.1 %all_gather.50 = bf16[1,32,8,896]{3,1,0,2:T(8,128)(2,1)S(1)} all-gather(bf16[1,32,2,896]{3,1,0,2:T(8,128)(2,1)S(1)} %copy.37), channel_id=1, replica_groups=mesh['expert'=32,'row'=4,'col'=4] {'col'}, dimensions={2}, use_global_device_ids=true | all-gather | bytes 573440 | tf_op jit(solution)/shard_map/all_gather | solution.py:16
  63.7 0.9 select_bitcast_fusion.1
  64.8 23.0 %all_to_all.30 = bf16[1,32,2,896]{3,2,0,1:T(2,128)(2,1)S(1)} all-to-all(bf16[1,32,2,896]{3,2,0,1:T(2,128)(2,1)S(1)} %get-tuple-element.20), channel_id=1, replica_groups=mesh['expert'=32,'row'=4,'col'=4] {'expert'}, dimensions={1} | all-to-all | bytes 229376 | tf_op jit(solution)/shard_map/all_to_all | solution.py:13
  87.8 11.1 %all_gather.48 = bf16[1,32,8,896]{3,1,0,2:T(8,128)(2,1)S(1)} all-gather(bf16[1,32,2,896]{3,1,0,2:T(8,128)(2,1)S(1)} %copy.34), channel_id=1, replica_groups=mesh['expert'=32,'row'=4,'col'=4] {'col'}, dimensions={2}, use_global_device_ids=true | all-gather | bytes 573440 | tf_op jit(solution)/shard_map/all_gather | solution.py:16
  98.9 0.9 select_bitcast_fusion.2
  99.9 23.0 %all_to_all.31 = bf16[1,32,2,896]{3,2,0,1:T(2,128)(2,1)S(1)} all-to-all(bf16[1,32,2,896]{3,2,0,1:T(2,128)(2,1)S(1)} %get-tuple-element.21), channel_id=1, replica_groups=mesh['expert'=32,'row'=4,'col'=4] {'expert'}, dimensions={1} | all-to-all | bytes 229376 | tf_op jit(solution)/shard_map/all_to_all | solution.py:13
  123.0 10.6 %all_gather.46 = bf16[1,32,8,896]{3,1,0,2:T(8,128)(2,1)S(1)} all-gather(bf16[1,32,2,896]{3,1,0,2:T(8,128)(2,1)S(1)} %copy.31), channel_id=1, replica_groups=mesh['expert'=32,'row'=4,'col'=4] {'col'}, dimensions={2}, use_global_device_ids=true | all-gather | bytes 573440 | tf_op jit(solution)/shard_map/all_gather | solution.py:16
  133.6 1.0 select_bitcast_fusion.3
  134.6 24.8 %all_to_all.32 = bf16[1,32,2,896]{3,2,0,1:T(2,128)(2,1)S(1)} all-to-all(bf16[1,32,2,896]{3,2,0,1:T(2,128)(2,1)S(1)} %get-tuple-element.22), channel_id=1, replica_groups=mesh['expert'=32,'row'=4,'col'=4] {'expert'}, dimensions={1} | all-to-all | bytes 229376 | tf_op jit(solution)/shard_map/all_to_all | solution.py:13
  159.4 11.3 %all_gather.44 = bf16[1,32,8,896]{3,1,0,2:T(8,128)(2,1)S(1)} all-gather(bf16[1,32,2,896]{3,1,0,2:T(8,128)(2,1)S(1)} %copy.28), channel_id=1, replica_groups=mesh['expert'=32,'row'=4,'col'=4] {'col'}, dimensions={2}, use_global_device_ids=true | all-gather | bytes 573440 | tf_op jit(solution)/shard_map/all_gather | solution.py:16
  170.8 0.9 select_bitcast_fusion.4
  171.8 19.4 %all_to_all.33 = bf16[1,32,2,896]{3,2,0,1:T(2,128)(2,1)S(1)} all-to-all(bf16[1,32,2,896]{3,2,0,1:T(2,128)(2,1)S(1)} %get-tuple-element.23), channel_id=1, replica_groups=mesh['expert'=32,'row'=4,'col'=4] {'expert'}, dimensions={1} | all-to-all | bytes 229376 | tf_op jit(solution)/shard_map/all_to_all | solution.py:13
  191.2 11.1 %all_gather.42 = bf16[1,32,8,896]{3,1,0,2:T(8,128)(2,1)S(1)} all-gather(bf16[1,32,2,896]{3,1,0,2:T(8,128)(2,1)S(1)} %copy.25), channel_id=1, replica_groups=mesh['expert'=32,'row'=4,'col'=4] {'col'}, dimensions={2}, use_global_device_ids=true | all-gather | bytes 573440 | tf_op jit(solution)/shard_map/all_gather | solution.py:16
  202.3 1.0 select_bitcast_fusion.5
  203.4 21.3 %all_to_all.34 = bf16[1,32,2,896]{3,2,0,1:T(2,128)(2,1)S(1)} all-to-all(bf16[1,32,2,896]{3,2,0,1:T(2,128)(2,1)S(1)} %get-tuple-element.18), channel_id=1, replica_groups=mesh['expert'=32,'row'=4,'col'=4] {'expert'}, dimensions={1} | all-to-all | bytes 229376 | tf_op jit(solution)/shard_map/all_to_all | solution.py:13
  224.7 11.5 %all_gather.52 = bf16[1,32,8,896]{3,1,0,2:T(8,128)(2,1)S(1)} all-gather(bf16[1,32,2,896]{3,1,0,2:T(8,128)(2,1)S(1)} %copy.40), channel_id=1, replica_groups=mesh['expert'=32,'row'=4,'col'=4] {'col'}, dimensions={2}, use_global_device_ids=true | all-gather | bytes 573440 | tf_op jit(solution)/shard_map/all_gather | solution.py:16
  236.3 0.9 select_bitcast_fusion
  237.2 0.6 dynamic_slice.3
  239.4 0.7 select_reduce_fusion
  240.7 2.7 reduce_sum.85
  243.4 2.7 reduce_sum.84
  246.0 2.8 reduce_sum.83
  248.8 32.0 %all-gather.9.cloned.1.call-done = bf16[4,1,256,896]{3,2,1,0:T(8,128)(2,1)} async-done(((bf16[1,1,256,896]{3,2,1,0:T(8,128)(2,1)}), bf16[4,1,256,896]{3,2,1,0:T(8,128)(2,1)}) %all-gather.9.cloned.1.call-update) | async-done | bytes 1835024 | tf_op jit(solution)/shard_map/all_gather | solution.py:9
  280.8 2.7 reduce_sum.82
  283.4 49.8 %all-gather.7.cloned.1.call-done = bf16[4,1,256,896]{3,2,1,0:T(8,128)(2,1)} async-done(((bf16[1,1,256,896]{3,2,1,0:T(8,128)(2,1)}), bf16[4,1,256,896]{3,2,1,0:T(8,128)(2,1)}) %all-gather.7.cloned.1.call-update) | async-done | bytes 1835024 | tf_op jit(solution)/shard_map/all_gather | solution.py:9
  333.2 2.7 reduce_sum.81
  335.9 3.4 fusion.9
  339.4 2.4 fusion.7
  341.7 2.4 fusion.5
  344.2 2.3 fusion.3
  346.5 2.4 fusion.1
  348.9 36.8 %all-gather.17.cloned.1.call-done = bf16[4,1,256,896]{3,2,1,0:T(8,128)(2,1)} async-done(((bf16[1,1,256,896]{3,2,1,0:T(8,128)(2,1)}), bf16[4,1,256,896]{3,2,1,0:T(8,128)(2,1)}) %all-gather.17.cloned.1.call-update) | async-done | bytes 1835024 | tf_op jit(solution)/shard_map/all_gather | solution.py:9
  385.7 2.0 reduce_sum.86
  387.7 8.4 %divide_bitcast_fusion = f32[1,896,896]{2,1,0:T(8,128)} fusion(f32[896,896]{1,0:T(8,128)} %fusion.1, f32[896,896]{1,0:T(8,128)} %fusion.3, f32[896,896]{1,0:T(8,128)} %fusion.5, f32[896,896]{1,0:T(8,128)} %fusion.9, f32[896,896]{1,0:T(8,128)} %fusion.7, bf16[256,896]{1,0:T(8,128)(2,1)S(1)} %reduce_sum.86, f32[]{:T(128)S(6)} %convert_element_type.2, ...), kind=kOutput, calls=%fused_computation.3 | convolution fusion | flops 415858688 | bytes 20185092 | tf_op jit(solution)/shard_map/kpa,kpb->ab/dot_general | solution.py:19
  (41 shorter events, 0.7 us)
Async XLA Ops:
  6.5 5.8 %copy-start = (bf16[256,896]{1,0:T(8,128)(2,1)S(1)}, bf16[256,896]{1,0:T(8,128)(2,1)}, u32[]{:S(2)}) copy-start(bf16[256,896]{1,0:T(8,128)(2,1)} %param.4) | copy-start | bytes 1376260
  17.0 35.6 %all-to-all-start.4 = ((bf16[1,32,2,896]{3,2,0,1:T(2,128)(2,1)}), bf16[1,32,2,896]{3,2,0,1:T(2,128)(2,1)S(1)}, u32[]{:S(2)}, u32[]{:S(2)}) async-start(bf16[1,32,2,896]{3,2,0,1:T(2,128)(2,1)} %get-tuple-element.19), calls=%async_computation.4 | async-start | bytes 229376 | tf_op jit(solution)/shard_map/all_to_all | solution.py:13
  36.2 204.5 %all-gather.15.cloned.1.call-start = ((), (), s32[]{:S(2)}) async-start(), calls=%async_computation.10 | async-start | bytes 2293760 | tf_op jit(solution)/shard_map/all_gather | solution.py:9
  64.7 178.7 %all-gather.13.cloned.1.call-start = ((), (), s32[]{:S(2)}) async-start(), calls=%async_computation.9 | async-start | bytes 2293760 | tf_op jit(solution)/shard_map/all_gather | solution.py:9
  99.8 146.2 %all-gather.11.cloned.1.call-start = ((), (), s32[]{:S(2)}) async-start(), calls=%async_computation.8 | async-start | bytes 2293760 | tf_op jit(solution)/shard_map/all_gather | solution.py:9
  134.6 146.2 %all-gather.9.cloned.1.call-start = ((), (), s32[]{:S(2)}) async-start(), calls=%async_computation.7 | async-start | bytes 2293760 | tf_op jit(solution)/shard_map/all_gather | solution.py:9
  170.8 68.7 %copy-start.5 = (s32[6,32]{1,0:T(8,128)S(1)}, s32[6,32]{1,0:T(8,128)}, u32[]{:S(2)}) copy-start(s32[6,32]{1,0:T(8,128)} %param.6) | copy-start | bytes 2308
  171.7 161.5 %all-gather.7.cloned.1.call-start = ((), (), s32[]{:S(2)}) async-start(), calls=%async_computation.6 | async-start | bytes 2293760 | tf_op jit(solution)/shard_map/all_gather | solution.py:9
  203.3 182.4 %all-gather.17.cloned.1.call-start = ((), (), s32[]{:S(2)}) async-start(), calls=%async_computation.11 | async-start | bytes 2293760 | tf_op jit(solution)/shard_map/all_gather | solution.py:9
  335.9 3.4 copy-start.4
  335.9 5.8 %copy-start.3 = (bf16[256,896]{1,0:T(8,128)(2,1)S(1)}, bf16[256,896]{1,0:T(8,128)(2,1)}, u32[]{:S(2)}) copy-start(bf16[256,896]{1,0:T(8,128)(2,1)} %reduce_sum.83) | copy-start | bytes 1376260
  339.4 4.8 %copy-start.2 = (bf16[256,896]{1,0:T(8,128)(2,1)S(1)}, bf16[256,896]{1,0:T(8,128)(2,1)}, u32[]{:S(2)}) copy-start(bf16[256,896]{1,0:T(8,128)(2,1)} %reduce_sum.84) | copy-start | bytes 1376260
  341.7 4.8 %copy-start.1 = (bf16[256,896]{1,0:T(8,128)(2,1)S(1)}, bf16[256,896]{1,0:T(8,128)(2,1)}, u32[]{:S(2)}) copy-start(bf16[256,896]{1,0:T(8,128)(2,1)} %reduce_sum.85) | copy-start | bytes 1376260
Sparse Core Ops, SparseCore 0:
  64.8 47.6 all-gather.14
  114.6 56.0 all-gather.12
  172.9 54.9 all-gather.10
  229.8 50.9 all-gather.8
  282.7 50.4 all-gather.6
  335.2 50.4 all-gather.16
